TPU v7x, 256 devices: a whole 4x4x8 slice. The times are simulated.
256 devices in a mesh: ctx: 64 (over x, z, y_hi), tp: 4 (over y_lo, core).
Axes of the slice: x: 4, y: 4 (y_hi: 2, y_lo: 2; y = y_hi * 2 + y_lo), z: 8, core: 2. Of those that a mesh axis runs over, the one named last changes fastest.
Arguments:
- q_one: bfloat16 [16384, 4096], P('ctx', 'tp'), may hold values from -880 to 880
- k_one: bfloat16 [16384, 4096], P('ctx', 'tp'), may hold values from -6 to 6
- v_one: bfloat16 [16384, 4096], P('ctx', 'tp'), may hold values from -6 to 6
- q_two: bfloat16 [16384, 4096], P('ctx', 'tp'), may hold values from -6 to 6
- k_two: bfloat16 [16384, 4096], P('ctx', 'tp'), may hold values from -6 to 6
- short_taps: bfloat16 [3, 7, 256], P(None, None, 'tp'), may hold values from -2 to 2
- medium_taps: bfloat16 [128, 256], P(None, 'tp'), may hold values from -0.5 to 0.5
- long_taps: bfloat16 [256, 16384], P('tp', 'ctx'), may hold values from -0.046875 to 0.046875
- skip_gain: float32 [4096], P('tp'), may hold values from -4 to 4
- block_order: int32 [64], replicated, may hold values from 0 to 63, as said below
- prev_owner: int32 [64], replicated, may hold values from 0 to 63, as said below
Outputs:
- gated_out: bfloat16 [16384, 4096], P('ctx', 'tp')
Inputs may be any that keep to these rules, and one draw needn't show every extreme that they name: `block_order`: A permutation of the 64 sequence blocks over the devices of ctx. prev_owner[b] is the device d with block_order[d] = b - 1 for b > 0, and prev_owner[0] the device holding block 63.
All inputs are finite; a program needn't handle non-finite values.
Results may differ from a plain program's by a relative error of at most 0.008.
Values may be sent and summed in bfloat16 or wider, within the bound.
A program may use at most 128 MiB of HBM per device.

v0:
```python
import math

import jax
import jax.numpy as jnp
from jax import lax
from jax.sharding import PartitionSpec as P

EPSILON = 1e-06
HIGHEST = lax.Precision.HIGHEST


def rows_filter(signal, kernel_taps):
    flipped = kernel_taps[::-1][:, None, :]
    result = lax.conv_general_dilated(
        signal[None],
        flipped,
        (1,),
        "VALID",
        dimension_numbers=("NWC", "WIO", "NWC"),
        feature_group_count=signal.shape[1],
        preferred_element_type=jnp.float32,
    )
    return result[0]


def angle_table(first_len, second_len, period):
    first = jnp.arange(first_len, dtype=jnp.int32)
    second = jnp.arange(second_len, dtype=jnp.int32)
    angle = 2.0 * math.pi / period * (first[:, None] * second[None, :] % period).astype(jnp.float32)
    return (jnp.cos(angle), jnp.sin(angle))


def forward_spectrum(signal, half_outer, tables):
    outer_cos, outer_sin, twist_cos, twist_sin, inner_cos, inner_sin = tables
    real_a = jnp.einsum("kn,bnm->bkm", outer_cos[:, :half_outer], signal, precision=HIGHEST)
    imag_a = -jnp.einsum("kn,bnm->bkm", outer_sin[:, :half_outer], signal, precision=HIGHEST)
    real_b = real_a * twist_cos + imag_a * twist_sin
    imag_b = imag_a * twist_cos - real_a * twist_sin
    real_c = jnp.einsum("bkm,mj->bkj", real_b, inner_cos, precision=HIGHEST) + jnp.einsum(
        "bkm,mj->bkj", imag_b, inner_sin, precision=HIGHEST
    )
    imag_c = jnp.einsum("bkm,mj->bkj", imag_b, inner_cos, precision=HIGHEST) - jnp.einsum(
        "bkm,mj->bkj", real_b, inner_sin, precision=HIGHEST
    )
    return (real_c, imag_c)


def inverse_spectrum(real_p, imag_p, half_outer, tables):
    outer_cos, outer_sin, twist_cos, twist_sin, inner_cos, inner_sin = tables
    real_q = jnp.einsum("bkj,jm->bkm", real_p, inner_cos, precision=HIGHEST) - jnp.einsum(
        "bkj,jm->bkm", imag_p, inner_sin, precision=HIGHEST
    )
    imag_q = jnp.einsum("bkj,jm->bkm", imag_p, inner_cos, precision=HIGHEST) + jnp.einsum(
        "bkj,jm->bkm", real_p, inner_sin, precision=HIGHEST
    )
    real_r = real_q * twist_cos - imag_q * twist_sin
    imag_r = imag_q * twist_cos + real_q * twist_sin
    return jnp.einsum(
        "nk,bkm->bnm", outer_cos[:half_outer], real_r, precision=HIGHEST
    ) - jnp.einsum("nk,bkm->bnm", outer_sin[:half_outer], imag_r, precision=HIGHEST)


def long_mix(values, long_rows, gain_local, block_rows):
    channels, length = values.shape
    outer_len = length // block_rows
    inner_len = 2 * block_rows
    half_outer = outer_len // 2
    padded_len = 2 * length
    outer_cos, outer_sin = angle_table(outer_len, outer_len, outer_len)
    twist_cos, twist_sin = angle_table(outer_len, inner_len, padded_len)
    inner_cos, inner_sin = angle_table(inner_len, inner_len, inner_len)
    tables = (outer_cos, outer_sin, twist_cos, twist_sin, inner_cos, inner_sin)
    value_float = values.astype(jnp.float32)
    real_x, imag_x = forward_spectrum(
        value_float.reshape(channels, half_outer, inner_len), half_outer, tables
    )
    real_h, imag_h = forward_spectrum(
        long_rows.astype(jnp.float32).reshape(long_rows.shape[0], half_outer, inner_len),
        half_outer,
        tables,
    )
    group_size = channels // long_rows.shape[0]
    real_h = jnp.repeat(real_h, group_size, axis=0)
    imag_h = jnp.repeat(imag_h, group_size, axis=0)
    real_p = real_x * real_h - imag_x * imag_h
    imag_p = real_x * imag_h + imag_x * real_h
    long_part = inverse_spectrum(real_p, imag_p, half_outer, tables) / padded_len
    return (long_part.reshape(channels, length) + gain_local[:, None] * value_float).astype(
        jnp.bfloat16
    )


def per_device(
    q_one,
    k_one,
    v_one,
    q_two,
    k_two,
    short_taps,
    medium_taps,
    long_taps,
    skip_gain,
    block_order,
    prev_owner,
):
    block_rows, local_width = q_one.shape
    ctx_count = lax.axis_size("ctx")
    device_pos = lax.axis_index("ctx")
    group_size = local_width // short_taps.shape[2]
    short_lead = short_taps.shape[1] - 1
    medium_reach = medium_taps.shape[0] - 1
    lane_width = local_width // ctx_count
    full_width = local_width * lax.axis_size("tp")
    short_lanes = jnp.repeat(short_taps, group_size, axis=2)
    medium_lanes = jnp.repeat(medium_taps, group_size, axis=1)
    lane_start = device_pos * lane_width
    slots = jnp.arange(ctx_count, dtype=jnp.int32)
    holder = jnp.sum(jnp.where(block_order[None, :] == slots[:, None], slots[None, :], 0), axis=1)
    my_block = block_order[device_pos]
    source = prev_owner[my_block]
    end_span = short_lead + medium_reach
    k_end = rows_filter(k_one[block_rows - end_span :], short_lanes[1])
    v_end = rows_filter(v_one[block_rows - end_span :], short_lanes[2])
    z_end = (k_end * v_end).astype(jnp.bfloat16)

    def select_source(carry, pieces):
        count = pieces[0].shape[0]
        matches = jnp.arange(count, dtype=jnp.int32) == source
        return tuple(
            (
                partial_sum
                + jnp.sum(jnp.where(matches[:, None, None], piece.astype(jnp.float32), 0.0), axis=0)
                for partial_sum, piece in zip(carry, pieces)
            )
        )

    empty_tails = (
        jnp.zeros((short_lead, local_width), jnp.float32),
        jnp.zeros((short_lead, local_width), jnp.float32),
        jnp.zeros((short_lead, local_width), jnp.float32),
        jnp.zeros((medium_reach, local_width), jnp.float32),
    )
    fetched = select_source(
        empty_tails,
        (
            lax.all_gather(q_one[None, block_rows - short_lead :], "ctx", axis=0, tiled=True),
            lax.all_gather(k_one[None, block_rows - short_lead :], "ctx", axis=0, tiled=True),
            lax.all_gather(v_one[None, block_rows - short_lead :], "ctx", axis=0, tiled=True),
            lax.all_gather(z_end[None], "ctx", axis=0, tiled=True),
        ),
    )
    has_before = my_block > 0
    tail_rows = [jnp.where(has_before, piece, 0.0).astype(jnp.bfloat16) for piece in fetched]
    q_feat = rows_filter(jnp.concatenate([tail_rows[0], q_one], axis=0), short_lanes[0])
    k_feat = rows_filter(jnp.concatenate([tail_rows[1], k_one], axis=0), short_lanes[1])
    v_feat = rows_filter(jnp.concatenate([tail_rows[2], v_one], axis=0), short_lanes[2])
    z_one = (k_feat * v_feat).astype(jnp.bfloat16)
    medium = rows_filter(jnp.concatenate([tail_rows[3], z_one], axis=0), medium_lanes)
    mixed = q_feat * medium
    energy = lax.psum(jnp.sum(mixed * mixed, axis=1), "tp")
    v_two = (
        k_two.astype(jnp.float32) * mixed * lax.rsqrt(energy / full_width + EPSILON)[:, None]
    ).astype(jnp.bfloat16)
    lanes, long_rows = (
        lax.all_to_all(jnp.transpose(v_two), "ctx", split_axis=0, concat_axis=1, tiled=True),
        lax.all_to_all(long_taps, "ctx", split_axis=0, concat_axis=1, tiled=True),
    )
    values = jnp.take(lanes.reshape(lane_width, ctx_count, block_rows), holder, axis=1).reshape(
        lane_width, ctx_count * block_rows
    )
    gain_local = lax.dynamic_slice_in_dim(skip_gain, lane_start, lane_width)
    mixed_seq = long_mix(values, long_rows, gain_local, block_rows)
    device_major = jnp.take(
        mixed_seq.reshape(lane_width, ctx_count, block_rows), block_order, axis=1
    ).reshape(lane_width, ctx_count * block_rows)
    returned = lax.all_to_all(device_major, "ctx", split_axis=1, concat_axis=0, tiled=True)
    return (q_two.astype(jnp.float32) * jnp.transpose(returned).astype(jnp.float32)).astype(
        jnp.bfloat16
    )


def solution(mesh):
    in_specs = (
        P("ctx", "tp"),
        P("ctx", "tp"),
        P("ctx", "tp"),
        P("ctx", "tp"),
        P("ctx", "tp"),
        P(None, None, "tp"),
        P(None, "tp"),
        P("tp", "ctx"),
        P("tp"),
        P(),
        P(),
    )
    out_specs = P("ctx", "tp")
    return jax.shard_map(
        per_device, mesh=mesh, in_specs=in_specs, out_specs=out_specs, check_vma=False
    )
```

profile of v0, /device:TPU:2, one launch (start us, length us, event | category | flops | bytes accessed | tf_op | source)
XLA Modules:
  0.0 769.9 jit_solution(8870785793664506424)
XLA Ops:
  8.4 1.0 slice_bitcast_fusion.1
  13.8 14.7 %all-to-all-start.1 = ((bf16[64,2,128]{2,1,0:T(2,128)(2,1)}), bf16[64,2,128]{2,1,0:T(2,128)(2,1)S(1)}, u32[]{:S(2)}, u32[]{:S(2)}) async-start(bf16[64,2,128]{2,1,0:T(2,128)(2,1)} %reshape.284), calls=%async_computation.1 | async-start | bytes 65536 | tf_op jit(solution)/shard_map/all_to_all | solution.py:166
  33.0 170.4 %all-gather.3 = bf16[64,6,1024]{2,1,0:T(8,128)(2,1)S(1)} all-gather(bf16[1,6,1024]{2,1,0:T(8,128)(2,1)S(1)} %slice_bitcast_fusion.9), channel_id=2, replica_groups=mesh['ctx'=64,'tp'=4] {'ctx'}, dimensions={0}, use_global_device_ids=true | all-gather | bytes 798720 | tf_op jit(solution)/shard_map/all_gather | solution.py:146
  203.4 172.6 %all-gather.4 = bf16[64,6,1024]{2,1,0:T(8,128)(2,1)S(1)} all-gather(bf16[1,6,1024]{2,1,0:T(8,128)(2,1)S(1)} %slice_bitcast_fusion.8), channel_id=3, replica_groups=mesh['ctx'=64,'tp'=4] {'ctx'}, dimensions={0}, use_global_device_ids=true | all-gather | bytes 798720 | tf_op jit(solution)/shard_map/all_gather | solution.py:147
  376.1 183.0 %all-gather.5 = bf16[64,6,1024]{2,1,0:T(8,128)(2,1)S(1)} all-gather(bf16[1,6,1024]{2,1,0:T(8,128)(2,1)S(1)} %slice_bitcast_fusion.7), channel_id=4, replica_groups=mesh['ctx'=64,'tp'=4] {'ctx'}, dimensions={0}, use_global_device_ids=true | all-gather | bytes 798720 | tf_op jit(solution)/shard_map/all_gather | solution.py:148
  566.4 1.3 reshape.270
  568.6 1.1 copy.125
  569.7 1.3 dynamic_slice.11
  573.2 7.4 select_reduce_fusion
  581.7 14.8 %fusion.32 = f32[1,256,1024]{2,0,1:T(1,128)S(1)} fusion(bf16[128,1,1024]{2,1,0:T(2,128)(2,1)S(1)} %copy-done.3, bf16[1,383,1024]{2,1,0:T(8,128)(2,1)S(1)} %maximum_bitcast_fusion, f32[1,264,1024]{2,0,1:T(1,128)S(1)} %reshape.270), kind=kOutput, calls=%fused_computation.55 | convolution fusion | flops 67371008 | bytes 3143680 | tf_op jit(solution)/shard_map/conv_general_dilated | solution.py:14
  596.7 5.8 psum.7
  602.5 1.2 fusion.82
  604.8 33.8 %all-to-all-start = ((bf16[64,16,256]{2,1,0:T(8,128)(2,1)}), bf16[64,16,256]{2,1,0:T(8,128)(2,1)S(1)}, u32[]{:S(2)}, u32[]{:S(2)}) async-start(bf16[64,16,256]{2,1,0:T(8,128)(2,1)} %bitcast.26), calls=%async_computation | async-start | bytes 1048576 | tf_op jit(solution)/shard_map/all_to_all | solution.py:165
  638.9 5.1 fusion.90
  644.0 5.1 fusion.88
  649.1 5.3 convolution_add_fusion.2
  654.4 5.1 convolution_subtract_fusion.2
  660.7 1.1 fusion.151
  661.8 1.1 fusion.153
  663.0 7.9 %fusion.52 = f32[16,64,512]{2,1,0:T(8,128)S(1)} fusion(f32[16,512,64]{1,2,0:T(8,128)S(1)} %fusion.153, f32[16,512,64]{1,2,0:T(8,128)S(1)} %fusion.151, f32[64,512]{1,0:T(8,128)S(1)} %get-tuple-element.14, f32[64,512]{1,0:T(8,128)S(1)} %get-tuple-element.15), kind=kOutput, calls=%fused_computation.76 | convolution fusion | flops 3226992640 | bytes 6553600 | tf_op jit(solution)/shard_map/bkm,mj->bkj/dot_general | solution.py:39
  670.9 7.7 %fusion.50 = f32[16,64,512]{2,1,0:T(8,128)S(1)} fusion(f32[16,512,64]{1,2,0:T(8,128)S(1)} %fusion.153, f32[16,512,64]{1,2,0:T(8,128)S(1)} %fusion.151, f32[64,512]{1,0:T(8,128)S(1)} %get-tuple-element.14, f32[64,512]{1,0:T(8,128)S(1)} %get-tuple-element.15), kind=kOutput, calls=%fused_computation.74 | convolution fusion | flops 3226992640 | bytes 6553600 | tf_op jit(solution)/shard_map/bkm,mj->bkj/dot_general | solution.py:42
  678.6 7.6 convolution_add_fusion.1
  686.2 7.8 %convolution_subtract_fusion.1 = f32[16,64,512]{2,1,0:T(8,128)S(1)} fusion(f32[16,64,512]{2,1,0:T(8,128)S(1)} %fusion.50, f32[16,512,64]{1,2,0:T(8,128)S(1)} %fusion.153, f32[16,512,64]{1,2,0:T(8,128)S(1)} %fusion.151, f32[64,512]{1,0:T(8,128)S(1)} %get-tuple-element.14, f32[64,512]{1,0:T(8,128)S(1)} %get-tuple-element.15), kind=kOutput, calls=%fused_computation.27 | convolution fusion | flops 3227516928 | bytes 8650752 | tf_op jit(solution)/shard_map/bkm,mj->bkj/dot_general | solution.py:42
  694.0 7.5 fusion.46
  701.6 8.0 %fusion.48 = f32[16,64,512]{2,1,0:T(8,128)S(1)} fusion(f32[16,64,512]{2,1,0:T(8,128)S(1)} %convolution_subtract_fusion.1, f32[16,64,512]{2,1,0:T(8,128)S(1)} %convolution_add_fusion.1, f32[64,512]{1,0:T(8,128)S(1)} %convolution_subtract_fusion.2, f32[64,512]{1,0:T(8,128)S(1)} %convolution_add_fusion.2), kind=kOutput, calls=%fused_computation.72 | convolution fusion | flops 3226468352 | bytes 6553600 | tf_op jit(solution)/shard_map/bkj,jm->bkm/dot_general | solution.py:50
  709.5 7.7 %convolution_add_fusion = f32[16,64,512]{2,1,0:T(8,128)S(1)} fusion(f32[16,64,512]{2,1,0:T(8,128)S(1)} %fusion.46, f32[16,64,512]{2,1,0:T(8,128)S(1)} %convolution_subtract_fusion.1, f32[16,64,512]{2,1,0:T(8,128)S(1)} %convolution_add_fusion.1, f32[64,512]{1,0:T(8,128)S(1)} %convolution_subtract_fusion.2, f32[64,512]{1,0:T(8,128)S(1)} %convolution_add_fusion.2), kind=kOutput, calls=%fused_computation.25 | convolution fusion | flops 3226992640 | bytes 8650752 | tf_op jit(solution)/shard_map/bkj,jm->bkm/dot_general | solution.py:53
  717.3 7.5 convolution_subtract_fusion
  724.8 1.6 fusion.5
  726.4 1.7 fusion.22
  731.1 12.8 %all-to-all-start.2 = ((bf16[16,64,256]{2,0,1:T(8,128)(2,1)}), bf16[16,64,256]{2,0,1:T(8,128)(2,1)S(1)}, u32[]{:S(2)}, u32[]{:S(2)}) async-start(bf16[16,64,256]{2,0,1:T(8,128)(2,1)} %select_bitcast_fusion), calls=%async_computation.2 | async-start | bytes 1048576 | tf_op jit(solution)/shard_map/all_to_all | solution.py:176
  744.1 17.6 %all-to-all-done.2 = bf16[16,64,256]{2,0,1:T(8,128)(2,1)S(1)} async-done(((bf16[16,64,256]{2,0,1:T(8,128)(2,1)}), bf16[16,64,256]{2,0,1:T(8,128)(2,1)S(1)}, u32[]{:S(2)}, u32[]{:S(2)}) %all-to-all-start.2) | async-done | bytes 524320 | tf_op jit(solution)/shard_map/all_to_all | solution.py:176
  761.9 1.0 copy.132
  (119 shorter events, 24.9 us)
Async XLA Ops:
  6.5 3.3 copy-start.1
  6.5 566.7 %all-gather.8.cloned.1.call-start = ((), (), s32[]{:S(2)}) async-start(), calls=%async_computation.3 | async-start | bytes 17039360 | tf_op jit(solution)/shard_map/all_gather | solution.py:149
  9.5 0.8 copy-start.11
  10.6 2.0 copy-start.5
  10.6 17.9 %copy-start.9 = (s32[64]{0:T(128)S(1)}, s32[64]{0:T(128)}, u32[]{:S(2)}) copy-start(s32[64]{0:T(128)} %param.22) | copy-start | bytes 772
  10.6 21.1 %copy-start.8 = (s32[64]{0:T(128)S(1)}, s32[64]{0:T(128)}, u32[]{:S(2)}) copy-start(s32[64]{0:T(128)} %param.23) | copy-start | bytes 772
  10.6 22.3 %copy-start = (bf16[256,1024]{1,0:T(8,128)(2,1)S(1)}, bf16[256,1024]{1,0:T(8,128)(2,1)}, u32[]{:S(2)}) copy-start(bf16[256,1024]{1,0:T(8,128)(2,1)} %param.15) | copy-start | bytes 1572868
  11.0 22.0 %copy-start.2 = (bf16[256,1024]{1,0:T(8,128)(2,1)S(1)}, bf16[256,1024]{1,0:T(8,128)(2,1)}, u32[]{:S(2)}) copy-start(bf16[256,1024]{1,0:T(8,128)(2,1)} %param.13) | copy-start | bytes 1572868
  13.8 558.9 %all-to-all-start.1 = ((bf16[64,2,128]{2,1,0:T(2,128)(2,1)}), bf16[64,2,128]{2,1,0:T(2,128)(2,1)S(1)}, u32[]{:S(2)}, u32[]{:S(2)}) async-start(bf16[64,2,128]{2,1,0:T(2,128)(2,1)} %reshape.284), calls=%async_computation.1 | async-start | bytes 65536 | tf_op jit(solution)/shard_map/all_to_all | solution.py:166
  561.0 0.7 copy-start.10
  565.8 2.0 copy-start.6
  580.6 1.0 copy-start.3
  604.8 54.8 %all-to-all-start = ((bf16[64,16,256]{2,1,0:T(8,128)(2,1)}), bf16[64,16,256]{2,1,0:T(8,128)(2,1)S(1)}, u32[]{:S(2)}, u32[]{:S(2)}) async-start(bf16[64,16,256]{2,1,0:T(8,128)(2,1)} %bitcast.26), calls=%async_computation | async-start | bytes 1048576 | tf_op jit(solution)/shard_map/all_to_all | solution.py:165
  728.1 0.7 copy-start.7
  729.6 14.3 %copy-start.4 = (bf16[256,1024]{1,0:T(8,128)(2,1)S(1)}, bf16[256,1024]{1,0:T(8,128)(2,1)}, u32[]{:S(2)}) copy-start(bf16[256,1024]{1,0:T(8,128)(2,1)} %param.16) | copy-start | bytes 1572868
  731.1 30.6 %all-to-all-start.2 = ((bf16[16,64,256]{2,0,1:T(8,128)(2,1)}), bf16[16,64,256]{2,0,1:T(8,128)(2,1)S(1)}, u32[]{:S(2)}, u32[]{:S(2)}) async-start(bf16[16,64,256]{2,0,1:T(8,128)(2,1)} %select_bitcast_fusion), calls=%async_computation.2 | async-start | bytes 1048576 | tf_op jit(solution)/shard_map/all_to_all | solution.py:176
Sparse Core Ops, SparseCore 0:
  12.1 213.6 all-gather.7
where the time goes:
time: 778 us; the launch traced here: 770 us
  blocking collectives  532 us (68%)
  matrix products  106 us (14%)
  starting transfers between devices  61.3 us (8%)
  local copies, waits for them, and re-layouts  20.6 us (3%)
  waiting for transfers between devices  17.7 us (2%)
  between operations  17 us (2%)
  other arithmetic  15.6 us (2%)
    all_gather x1, blocking collectives, per_device(): lax.all_gather(v_one[None, block_rows - short_lead:], 'ctx', axis=0, tile...  183 us
    all_gather x1, blocking collectives, per_device(): lax.all_gather(k_one[None, block_rows - short_lead:], 'ctx', axis=0, tile...  173 us
    all_gather x1, blocking collectives, per_device(): lax.all_gather(q_one[None, block_rows - short_lead:], 'ctx', axis=0, tile...  170 us
    all_to_all x1, starting transfers between devices, per_device(): lax.all_to_all(jnp.transpose(v_two), 'ctx', split_axis=0, concat_axis=1,...  33.8 us
    all_to_all x1, waiting for transfers between devices, per_device(): lax.all_to_all(device_major, 'ctx', split_axis=1, concat_axis=0, tiled=True)  17.6 us
    conv_general_dilated x6, matrix products, rows_filter(): lax.conv_general_dilated(signal[None], flipped, (1,), 'VALID', dimension_...  17.3 us
  transfers between devices with their start and end apart: 4, of which 1 were waited for; matrix products, arithmetic and copies ran while one was open for 5% of the time, Pallas kernels for 0%

commit v1 on v0

v1 whole, which is shorter than its diff:
```python
import functools

import jax
import jax.numpy as jnp
from jax import lax
from jax.experimental import pallas as pl
from jax.experimental.pallas import tpu as pltpu
from jax.sharding import PartitionSpec as P

EPSILON = 1e-06
LANES = 128
GROUP = 16
F32 = jnp.float32
BF16 = jnp.bfloat16
VMEM_LIMIT = 60 * 1024 * 1024


def iota(shape, dim):
    return lax.broadcasted_iota(jnp.int32, shape, dim)


def spread_taps(taps, tile):
    groups = taps.shape[1]
    pick = iota((groups, LANES), 0) == tile * (LANES // GROUP) + iota((groups, LANES), 1) // GROUP
    return jnp.dot(taps.astype(F32), pick.astype(F32), preferred_element_type=F32)


def skewed(row):
    return pltpu.roll(jnp.broadcast_to(row, (LANES, LANES)), 0, 1, stride=1, stride_axis=0)


def tail_kernel(q_ref, k_ref, v_ref, short_ref, out_ref):
    rows = k_ref.shape[0]
    lead = short_ref.shape[1] - 1
    start = rows - LANES - 8

    def tile_step(tile, _):
        lanes = pl.ds(pl.multiple_of(tile * LANES, LANES), LANES)
        features = []
        for which, ref in ((1, k_ref), (2, v_ref)):
            taps = spread_taps(short_ref[which], tile)
            signal = ref[pl.ds(start, LANES + 8), lanes].astype(F32)
            total = jnp.zeros((LANES, LANES), F32)
            for j in range(lead + 1):
                total += signal[8 - j : 8 - j + LANES] * taps[j : j + 1]
            features.append(total)
        z_tail = (features[0] * features[1]).astype(BF16)
        ends = [ref[pl.ds(rows - 8, 8), lanes].astype(F32)[8 - lead :] for ref in (q_ref, k_ref, v_ref)]
        ends = jnp.concatenate(ends + [jnp.zeros((6, LANES), F32)], axis=0)
        for a in range(8):
            out_ref[a * 8 + tile, 0:16, :] = z_tail[16 * a : 16 * a + 16]
            piece = jnp.concatenate([ends[3 * a : 3 * a + 3], jnp.zeros((5, LANES), F32)], axis=0)
            out_ref[a * 8 + tile, 16:24, :] = piece.astype(BF16)
        return 0

    lax.fori_loop(0, k_ref.shape[1] // LANES, tile_step, 0)


def mix_kernel(flag_ref, q_ref, k_ref, v_ref, k_two_ref, short_ref, medium_ref, tail_ref, out_ref, energy_ref, toeplitz, signal, z_pad):
    rows, width = q_ref.shape
    lead = short_ref.shape[1] - 1
    before = (flag_ref[0] > 0).astype(F32)
    reach = medium_ref.shape[0]
    flip = (iota((reach, reach), 0) == (reach - iota((reach, reach), 1)) % reach).astype(F32)
    turned = lax.dot_general(medium_ref[...].astype(F32), flip, (((0,), (0,)), ((), ())), preferred_element_type=F32)
    z_pad_groups = turned.shape[0]
    row_at, col_at = iota((LANES, LANES), 0), iota((LANES, LANES), 1)

    def tile_step(tile, energy):
        lanes = pl.ds(pl.multiple_of(tile * LANES, LANES), LANES)
        ends = jnp.concatenate([tail_ref[a * 8 + tile].astype(F32)[16:19] for a in range(6)], axis=0) * before
        features = []
        for which, ref in enumerate((q_ref, k_ref, v_ref)):
            taps = spread_taps(short_ref[which], tile)
            signal[0:8, :] = jnp.concatenate([jnp.zeros((8 - lead, LANES), F32), ends[which * lead : (which + 1) * lead]], axis=0)
            signal[8 : 8 + rows, :] = ref[:, lanes].astype(F32)
            total = jnp.zeros((rows, LANES), F32)
            for j in range(lead + 1):
                total += signal[8 - j : 8 - j + rows, :] * taps[j : j + 1]
            features.append(total)
        for a in range(8):
            z_pad[16 * a : 16 * a + 16, :] = (tail_ref[a * 8 + tile].astype(F32)[0:16] * before).astype(BF16)
        z_pad[LANES : LANES + rows, :] = (features[1] * features[2]).astype(BF16)
        picked = (iota((z_pad_groups, LANES), 0) // 8 == tile)
        for g in range(8):
            row = jnp.sum(jnp.where(iota((z_pad_groups, LANES), 0) == tile * 8 + g, turned, 0.0), axis=0, keepdims=True)
            skew = skewed(row)
            toeplitz[g * LANES : (g + 1) * LANES, 0:LANES] = jnp.where(col_at > row_at, skew, 0.0).astype(BF16)
            toeplitz[g * LANES : (g + 1) * LANES, LANES : 2 * LANES] = jnp.where(col_at <= row_at, skew, 0.0).astype(BF16)
        stacked = jnp.concatenate([z_pad[0:rows, :], z_pad[LANES : LANES + rows, :]], axis=1)
        product = jnp.dot(toeplitz[...], stacked, preferred_element_type=F32)
        owner = iota((LANES, 2 * LANES), 1) % LANES // GROUP
        medium = jnp.zeros((LANES, 2 * LANES), F32)
        for g in range(8):
            medium = jnp.where(owner == g, product[g * LANES : (g + 1) * LANES], medium)
        medium = jnp.concatenate([medium[:, :LANES], medium[:, LANES:]], axis=0)
        mixed = features[0] * medium
        out_ref[lanes, :] = jnp.transpose(mixed * k_two_ref[:, lanes].astype(F32))
        return energy + mixed * mixed

    energy = lax.fori_loop(0, width // LANES, tile_step, jnp.zeros((rows, LANES), F32))
    energy_ref[...] = jnp.sum(jnp.transpose(energy), axis=0, keepdims=True)


def long_kernel(holder_ref, order_ref, x_ref, taps_ref, gain_ref, out_ref, x_pad, toeplitz, total):
    blocks, channels, span = x_ref.shape
    size = blocks * channels
    quarter = size // 4
    x_pad[0:quarter, :] = jnp.zeros((quarter, span), BF16)

    def place(i, _):
        x_pad[pl.ds(pl.multiple_of(quarter + i * channels, channels), channels), :] = x_ref[holder_ref[i]]
        return 0

    lax.fori_loop(0, blocks, place, 0)
    row_at, col_at = iota((LANES, LANES), 0), iota((LANES, LANES), 1)
    toeplitz[:, 0:LANES] = jnp.zeros((LANES, LANES), BF16)

    def spread(k, last):
        row = taps_ref[k].astype(F32)
        first, second = skewed(row[:, :LANES]), skewed(row[:, LANES:])
        at = pl.multiple_of(LANES + k * span, LANES)
        toeplitz[:, pl.ds(at, LANES)] = jnp.where(col_at >= row_at, first, last).astype(BF16)
        toeplitz[:, pl.ds(at + LANES, LANES)] = jnp.where(col_at >= row_at, second, first).astype(BF16)
        return second

    lax.fori_loop(0, blocks, spread, jnp.zeros((LANES, LANES), F32))
    gain = gain_ref[...]
    step = 4
    for r in range(4):
        base = quarter * (r + 1)
        own = x_pad[base : base + quarter, :].astype(F32).reshape(quarter // channels, channels, span)
        total[...] = (own * gain[None]).reshape(quarter, span)

        def add(n, _):
            left, right = [], []
            for s in range(step):
                k = n * step + s
                left.append(x_pad[pl.ds(pl.multiple_of(base - k * channels, channels), quarter), :])
                at = pl.multiple_of(LANES + k * span, LANES)
                right.append(toeplitz[:, pl.ds(at, span)])
                right.append(toeplitz[:, pl.ds(pl.multiple_of(at - LANES, LANES), span)])
            total[...] += jnp.dot(jnp.concatenate(left, axis=1), jnp.concatenate(right, axis=0), preferred_element_type=F32)
            return 0

        lax.fori_loop(0, (r + 1) * (quarter // channels) // step, add, 0)
        out_ref[r * (quarter // channels) : (r + 1) * (quarter // channels)] = total[...].astype(BF16).reshape(quarter // channels, channels, span)


def gate_kernel(y_ref, q_two_ref, out_ref):
    blocks, channels, span = y_ref.shape
    per_tile = LANES // channels

    def tile_step(tile, _):
        lanes = pl.ds(pl.multiple_of(tile * LANES, LANES), LANES)
        piece = y_ref[pl.ds(tile * per_tile, per_tile)].astype(F32).reshape(LANES, span)
        out_ref[:, lanes] = (jnp.transpose(piece) * q_two_ref[:, lanes].astype(F32)).astype(BF16)
        return 0

    lax.fori_loop(0, q_two_ref.shape[1] // LANES, tile_step, 0)


VM = pl.BlockSpec(memory_space=pltpu.VMEM)
SM = pl.BlockSpec(memory_space=pltpu.SMEM)
PARAMS = pltpu.CompilerParams(vmem_limit_bytes=VMEM_LIMIT)


def per_device(q_one, k_one, v_one, q_two, k_two, short_taps, medium_taps, long_taps, skip_gain, block_order, prev_owner):
    rows, width = q_one.shape
    ctx_count = lax.axis_size("ctx")
    me = lax.axis_index("ctx")
    lane_width = width // ctx_count
    full_width = width * lax.axis_size("tp")
    slots = jnp.arange(ctx_count, dtype=jnp.int32)
    holder = jnp.sum(jnp.where(block_order[None, :] == slots[:, None], slots[None, :], 0), axis=1)
    source = prev_owner[block_order]

    long_rows = lax.all_to_all(long_taps, "ctx", split_axis=0, concat_axis=0, tiled=True).reshape(ctx_count, 1, rows)
    tails = pl.pallas_call(
        tail_kernel,
        out_shape=jax.ShapeDtypeStruct((ctx_count, 24, LANES), BF16),
        in_specs=[VM] * 4,
        out_specs=VM,
        compiler_params=PARAMS,
        name="tails",
    )(q_one, k_one, v_one, short_taps)
    spread = lax.all_to_all(tails, "ctx", split_axis=0, concat_axis=0, tiled=True)
    fetched = lax.all_to_all(jnp.take(spread, source, axis=0), "ctx", split_axis=0, concat_axis=0, tiled=True)
    flag = block_order[me].reshape(1)
    mixed, energy = pl.pallas_call(
        mix_kernel,
        out_shape=(jax.ShapeDtypeStruct((width, rows), F32), jax.ShapeDtypeStruct((1, rows), F32)),
        in_specs=[SM] + [VM] * 7,
        out_specs=(VM, VM),
        scratch_shapes=[
            pltpu.VMEM((8 * LANES, 2 * LANES), BF16),
            pltpu.VMEM((8 + rows, LANES), F32),
            pltpu.VMEM((LANES + rows, LANES), BF16),
        ],
        compiler_params=PARAMS,
        name="mix",
    )(flag, q_one, k_one, v_one, k_two, short_taps, medium_taps, fetched)
    energy = lax.psum(energy, "tp")
    v_two = (mixed * lax.rsqrt(energy / full_width + EPSILON)).astype(BF16)
    received = lax.all_to_all(v_two.reshape(ctx_count, lane_width, rows), "ctx", split_axis=0, concat_axis=0, tiled=True)
    gain = lax.dynamic_slice_in_dim(skip_gain, me * lane_width, lane_width).reshape(lane_width, 1)
    size = ctx_count * lane_width
    mixed_seq = pl.pallas_call(
        long_kernel,
        out_shape=jax.ShapeDtypeStruct((ctx_count, lane_width, rows), BF16),
        in_specs=[SM] * 2 + [VM] * 3,
        out_specs=VM,
        scratch_shapes=[
            pltpu.VMEM((size + size // 4, rows), BF16),
            pltpu.VMEM((LANES, LANES + ctx_count * rows), BF16),
            pltpu.VMEM((size // 4, rows), F32),
        ],
        compiler_params=PARAMS,
        name="long",
    )(holder, block_order, received, long_rows, gain)
    returned = lax.all_to_all(jnp.take(mixed_seq, block_order, axis=0), "ctx", split_axis=0, concat_axis=0, tiled=True)
    return pl.pallas_call(
        gate_kernel,
        out_shape=jax.ShapeDtypeStruct((rows, width), BF16),
        in_specs=[VM] * 2,
        out_specs=VM,
        compiler_params=PARAMS,
        name="gate",
    )(returned, q_two)


def solution(mesh):
    in_specs = (
        P("ctx", "tp"),
        P("ctx", "tp"),
        P("ctx", "tp"),
        P("ctx", "tp"),
        P("ctx", "tp"),
        P(None, None, "tp"),
        P(None, "tp"),
        P("tp", "ctx"),
        P("tp"),
        P(),
        P(),
    )
    return jax.shard_map(per_device, mesh=mesh, in_specs=in_specs, out_specs=P("ctx", "tp"), check_vma=False)
```

time: 778 us -> 166 us (0.21)
  blocking collectives: 532 us -> 30.3 us
  matrix products: 106 us -> 0 us
  Pallas kernels: 0 us -> 37.9 us
  waiting for transfers between devices: 17.7 us -> 42.9 us
  starting transfers between devices: 61.3 us -> 41.1 us
  between operations: 17 us -> 0.15 us
  local copies, waits for them, and re-layouts: 20.6 us -> 8.39 us
  other arithmetic: 15.6 us -> 4.5 us
    all_gather x3 -> x0, blocking collectives: 526 us -> none  [the longest x1 183 us: per_device(): lax.all_gather(v_one[None, block_rows - short_lead:], 'ctx', axis=0, tile...]
    dot_general x18 -> x0, matrix products: 88.5 us -> none  [the longest x2 13 us: forward_spectrum(): jnp.einsum('bkm,mj->bkj', real_b, inner_cos, precision=HIGHEST)]
    pallas_call x0 -> x4, Pallas kernels: none -> 37.9 us  [the longest x1 21.8 us: per_device(): pl.pallas_call(long_kernel, out_shape=jax.ShapeDtypeStruct((ctx_count, la...]
    all_to_all x3 -> x4, waiting for transfers between devices: 17.6 us -> 42.9 us  [the longest x1 16.1 us: per_device(): lax.all_to_all(v_two.reshape(ctx_count, lane_width, rows), 'ctx', split_a...]
    all_to_all x0 -> x1, blocking collectives: none -> 24.7 us  [per_device(): lax.all_to_all(jnp.take(mixed_seq, block_order, axis=0), 'ctx', split_axi...]
    all_to_all x3 -> x4, starting transfers between devices: 61.3 us -> 41.1 us  [the longest x1 14.8 us: per_device(): lax.all_to_all(tails, 'ctx', split_axis=0, concat_axis=0, tiled=True)]
    conv_general_dilated x6 -> x0, matrix products: 17.3 us -> none  [rows_filter(): lax.conv_general_dilated(signal[None], flipped, (1,), 'VALID', dimension_...]
    reduce_sum x3 -> x0, other arithmetic: 8.65 us -> none  [the longest x2 8.43 us: select_source(): jnp.sum(jnp.where(matches[:, None, None], piece.astype(jnp.float32), 0.0)...]
  transfers between devices with their start and end apart: 4 -> 4, of which waited for: 1 -> 3; matrix products, arithmetic and copies ran while one was open for 5% -> 5% of each run, Pallas kernels for 0% -> 6%
where the time goes in v1:
time: 166 us; the launch traced here: 165 us
  waiting for transfers between devices  42.9 us (26%)
  starting transfers between devices  41.1 us (25%)
  Pallas kernels  37.9 us (23%)
  blocking collectives  30.3 us (18%)
  local copies, waits for them, and re-layouts  8.39 us (5%)
  other arithmetic  4.5 us (3%)
    all_to_all x1, blocking collectives, per_device(): lax.all_to_all(jnp.take(mixed_seq, block_order, axis=0), 'ctx', split_axi...  24.7 us
    pallas_call x1, Pallas kernels, per_device(): pl.pallas_call(long_kernel, out_shape=jax.ShapeDtypeStruct((ctx_count, la...  21.8 us
    all_to_all x1, waiting for transfers between devices, per_device(): lax.all_to_all(v_two.reshape(ctx_count, lane_width, rows), 'ctx', split_a...  16.1 us
    all_to_all x1, waiting for transfers between devices, per_device(): lax.all_to_all(tails, 'ctx', split_axis=0, concat_axis=0, tiled=True)  14.8 us
    all_to_all x1, starting transfers between devices, per_device(): lax.all_to_all(tails, 'ctx', split_axis=0, concat_axis=0, tiled=True)  14.8 us
    all_to_all x1, starting transfers between devices, per_device(): lax.all_to_all(v_two.reshape(ctx_count, lane_width, rows), 'ctx', split_a...  12.7 us
    all_to_all x1, waiting for transfers between devices, per_device(): lax.all_to_all(jnp.take(spread, source, axis=0), 'ctx', split_axis=0, con...  12 us
    pallas_call x1, Pallas kernels, per_device(): pl.pallas_call(mix_kernel, out_shape=(jax.ShapeDtypeStruct((width, rows),...  9.23 us
  transfers between devices with their start and end apart: 4, of which 3 were waited for; matrix products, arithmetic and copies ran while one was open for 5% of the time, Pallas kernels for 6%

profile of v1, /device:TPU:2, one launch (start us, length us, event | category | flops | bytes accessed | tf_op | source)
XLA Modules:
  0.0 165.3 jit_solution(15578807778043469865)
XLA Ops:
  0.0 4.1 %tails.1 = bf16[64,24,128]{2,1,0:T(8,128)(2,1)} custom-call(bf16[256,1024]{1,0:T(8,128)(2,1)} %q_ref.3, bf16[256,1024]{1,0:T(8,128)(2,1)} %k_ref.3, bf16[256,1024]{1,0:T(8,128)(2,1)} %v_ref.3, bf16[3,7,64]{2,1,0:T(8,128)(2,1)} %short_ref.3), custom_call_target="tpu_custom_call" | custom-call | tf_op jit(solution)/shard_map/tails/pallas_call | solution.py:179
  4.1 14.8 %all-to-all-start = ((bf16[64,24,128]{2,1,0:T(8,128)(2,1)}), bf16[64,24,128]{2,1,0:T(8,128)(2,1)S(1)}, u32[]{:S(2)}, u32[]{:S(2)}) async-start(bf16[64,24,128]{2,1,0:T(8,128)(2,1)} %tails.1), calls=%async_computation | async-start | bytes 786432 | tf_op jit(solution)/shard_map/all_to_all | solution.py:187
  18.9 0.8 gather_fusion
  19.7 14.8 %all-to-all-done = bf16[64,24,128]{2,1,0:T(8,128)(2,1)S(1)} async-done(((bf16[64,24,128]{2,1,0:T(8,128)(2,1)}), bf16[64,24,128]{2,1,0:T(8,128)(2,1)S(1)}, u32[]{:S(2)}, u32[]{:S(2)}) %all-to-all-start) | async-done | bytes 393248 | tf_op jit(solution)/shard_map/all_to_all | solution.py:187
  34.5 0.6 gather_fusion.1
  35.2 0.9 broadcast_select_fusion.1
  36.1 6.8 %all-to-all-start.1 = ((bf16[64,24,128]{2,1,0:T(8,128)(2,1)}), bf16[64,24,128]{2,1,0:T(8,128)(2,1)S(1)}, u32[]{:S(2)}, u32[]{:S(2)}) async-start(bf16[64,24,128]{2,1,0:T(8,128)(2,1)} %broadcast_select_fusion.1), calls=%async_computation.1 | async-start | bytes 786432 | tf_op jit(solution)/shard_map/all_to_all | solution.py:188
  42.9 0.0 copy-start.4
  42.9 0.6 dynamic_slice.6.flag_ref
  43.5 0.7 copy.17.medium_ref
  44.2 0.5 broadcast.39
  44.8 0.6 reduce
  45.4 0.6 reshape.62
  46.0 12.0 %all-to-all-done.1.tail_ref = bf16[64,24,128]{2,1,0:T(8,128)(2,1)S(1)} async-done(((bf16[64,24,128]{2,1,0:T(8,128)(2,1)}), bf16[64,24,128]{2,1,0:T(8,128)(2,1)S(1)}, u32[]{:S(2)}, u32[]{:S(2)}) %all-to-all-start.1) | async-done | bytes 393248 | tf_op jit(solution)/shard_map/all_to_all | solution.py:188
  58.0 6.7 %all-to-all-start.3 = ((bf16[64,2,128]{2,1,0:T(2,128)(2,1)}), bf16[64,2,128]{2,1,0:T(2,128)(2,1)S(1)}, u32[]{:S(2)}, u32[]{:S(2)}) async-start(bf16[64,2,128]{2,1,0:T(2,128)(2,1)} %reshape.62), calls=%async_computation.3 | async-start | bytes 65536 | tf_op jit(solution)/shard_map/all_to_all | solution.py:178
  64.8 9.2 %mix.1 = (f32[1024,256]{1,0:T(8,128)}, f32[1,256]{1,0:T(1,128)}) custom-call(s32[1]{0:T(128)} %dynamic_slice.6.flag_ref, bf16[256,1024]{1,0:T(8,128)(2,1)} %q_ref.3, bf16[256,1024]{1,0:T(8,128)(2,1)} %k_ref.3, bf16[256,1024]{1,0:T(8,128)(2,1)} %v_ref.3, bf16[256,1024]{1,0:T(8,128)(2,1)} %k_two_ref.1, bf16[3,7,64]{2,1,0:T(8,128)(2,1)} %short_ref.3, ...), custom_call_target="tpu_custom_call" | custom-call | tf_op jit(solution)/shard_map/mix/pallas_call | solution.py:190
  74.0 0.7 copy-done.6
  74.7 5.6 %psum.7 = f32[1,256]{1,0:T(1,128)S(1)} all-reduce(f32[1,256]{1,0:T(1,128)S(1)} %copy-done.6), channel_id=1, replica_groups=mesh['ctx'=64,'tp'=4] {'tp'}, use_global_device_ids=true, to_apply=%region_1.2 | all-reduce | flops 256 | bytes 2048 | tf_op jit(solution)/shard_map/psum | solution.py:203
  80.3 2.1 %multiply_convert_fusion = bf16[1024,256]{1,0:T(8,128)(2,1)} fusion(f32[1024,256]{1,0:T(8,128)} %get-tuple-element.7, f32[256]{0:T(256)S(1)} %bitcast.10), kind=kLoop, calls=%fused_computation.3 | loop fusion | flops 524288 | bytes 1573888 | tf_op jit(solution)/shard_map/convert_element_type | solution.py:204
  82.4 0.0 all-to-all-done.3
  82.4 12.7 %all-to-all-start.2 = ((bf16[64,16,256]{2,1,0:T(8,128)(2,1)}), bf16[64,16,256]{2,1,0:T(8,128)(2,1)S(1)}, u32[]{:S(2)}, u32[]{:S(2)}) async-start(bf16[64,16,256]{2,1,0:T(8,128)(2,1)} %bitcast.3), calls=%async_computation.2 | async-start | bytes 1048576 | tf_op jit(solution)/shard_map/all_to_all | solution.py:205
  95.2 0.1 dynamic-slice_bitcast_fusion
  95.2 0.7 copy.19.gain_ref
  95.9 0.7 select_reduce_fusion.holder_ref
  96.6 0.6 reshape.63.taps_ref
  97.2 16.1 %all-to-all-done.2.x_ref = bf16[64,16,256]{2,1,0:T(8,128)(2,1)S(1)} async-done(((bf16[64,16,256]{2,1,0:T(8,128)(2,1)}), bf16[64,16,256]{2,1,0:T(8,128)(2,1)S(1)}, u32[]{:S(2)}, u32[]{:S(2)}) %all-to-all-start.2) | async-done | bytes 524320 | tf_op jit(solution)/shard_map/all_to_all | solution.py:205
  113.4 0.8 copy-done.2
  114.2 21.8 %long.1 = bf16[64,16,256]{2,1,0:T(8,128)(2,1)} custom-call(s32[64]{0:T(128)} %select_reduce_fusion.holder_ref, s32[64]{0:T(128)} %order_ref.1, bf16[64,16,256]{2,1,0:T(8,128)(2,1)} %copy-done.2, bf16[64,1,256]{2,1,0:T(2,128)(2,1)} %reshape.63.taps_ref, f32[16,1]{1,0:T(8,128)} %copy.19.gain_ref), custom_call_target="tpu_custom_call" | custom-call | tf_op jit(solution)/shard_map/long/pallas_call | solution.py:208
  136.0 1.6 gather_fusion.2
  137.6 0.1 broadcast_select_fusion
  137.8 24.7 %all_to_all.29.y_ref = bf16[64,16,256]{2,1,0:T(8,128)(2,1)} all-to-all(bf16[64,16,256]{2,1,0:T(8,128)(2,1)S(1)} %broadcast_select_fusion), channel_id=1, replica_groups=mesh['ctx'=64,'tp'=4] {'ctx'}, dimensions={0} | all-to-all | bytes 1048576 | tf_op jit(solution)/shard_map/all_to_all | solution.py:221
  162.5 2.8 %gate.1 = bf16[256,1024]{1,0:T(8,128)(2,1)} custom-call(bf16[64,16,256]{2,1,0:T(8,128)(2,1)} %all_to_all.29.y_ref, bf16[256,1024]{1,0:T(8,128)(2,1)} %q_two_ref.1), custom_call_target="tpu_custom_call" | custom-call | tf_op jit(solution)/shard_map/gate/pallas_call | solution.py:222
  (20 shorter events, 0.1 us)
Async XLA Ops:
  0.0 95.2 %copy-start = (f32[1024]{0:T(1024)S(1)}, f32[1024]{0:T(1024)}, u32[]{:S(2)}) copy-start(f32[1024]{0:T(1024)} %param.19) | copy-start | bytes 12292
  4.1 14.8 %copy-start.7 = (s32[64]{0:T(128)S(1)}, s32[64]{0:T(128)}, u32[]{:S(2)}) copy-start(s32[64]{0:T(128)} %order_ref.1) | copy-start | bytes 772
  4.1 14.8 %copy-start.1 = (s32[64]{0:T(128)S(1)}, s32[64]{0:T(128)}, u32[]{:S(2)}) copy-start(s32[64]{0:T(128)} %param.21) | copy-start | bytes 772
  4.1 30.4 %all-to-all-start = ((bf16[64,24,128]{2,1,0:T(8,128)(2,1)}), bf16[64,24,128]{2,1,0:T(8,128)(2,1)S(1)}, u32[]{:S(2)}, u32[]{:S(2)}) async-start(bf16[64,24,128]{2,1,0:T(8,128)(2,1)} %tails.1), calls=%async_computation | async-start | bytes 786432 | tf_op jit(solution)/shard_map/all_to_all | solution.py:187
  36.1 7.4 %copy-start.5 = (bf16[128,64]{0,1:T(8,128)(2,1)S(1)}, bf16[128,64]{0,1:T(8,128)(2,1)}, u32[]{:S(2)}) copy-start(bf16[128,64]{0,1:T(8,128)(2,1)} %param.17) | copy-start | bytes 49156
  36.1 21.9 %all-to-all-start.1 = ((bf16[64,24,128]{2,1,0:T(8,128)(2,1)}), bf16[64,24,128]{2,1,0:T(8,128)(2,1)S(1)}, u32[]{:S(2)}, u32[]{:S(2)}) async-start(bf16[64,24,128]{2,1,0:T(8,128)(2,1)} %broadcast_select_fusion.1), calls=%async_computation.1 | async-start | bytes 786432 | tf_op jit(solution)/shard_map/all_to_all | solution.py:188
  42.9 1.8 %copy-start.4 = (bf16[64,256]{1,0:T(8,128)(2,1)S(1)}, bf16[64,256]{1,0:T(8,128)(2,1)}, u32[]{:S(2)}) copy-start(bf16[64,256]{1,0:T(8,128)(2,1)} %param.18) | copy-start | bytes 98308
  58.0 6.8 %copy-start.3 = (bf16[64,24,128]{2,1,0:T(8,128)(2,1)}, bf16[64,24,128]{2,1,0:T(8,128)(2,1)S(1)}, u32[]{:S(2)}) copy-start(bf16[64,24,128]{2,1,0:T(8,128)(2,1)S(1)} %all-to-all-done.1.tail_ref) | copy-start | bytes 1179652
  58.0 24.4 %all-to-all-start.3 = ((bf16[64,2,128]{2,1,0:T(2,128)(2,1)}), bf16[64,2,128]{2,1,0:T(2,128)(2,1)S(1)}, u32[]{:S(2)}, u32[]{:S(2)}) async-start(bf16[64,2,128]{2,1,0:T(2,128)(2,1)} %reshape.62), calls=%async_computation.3 | async-start | bytes 65536 | tf_op jit(solution)/shard_map/all_to_all | solution.py:178
  74.0 0.7 copy-start.6
  82.4 31.0 %all-to-all-start.2 = ((bf16[64,16,256]{2,1,0:T(8,128)(2,1)}), bf16[64,16,256]{2,1,0:T(8,128)(2,1)S(1)}, u32[]{:S(2)}, u32[]{:S(2)}) async-start(bf16[64,16,256]{2,1,0:T(8,128)(2,1)} %bitcast.3), calls=%async_computation.2 | async-start | bytes 1048576 | tf_op jit(solution)/shard_map/all_to_all | solution.py:205
  113.4 0.8 copy-start.2

commit v2 on v1

v2 whole, which is shorter than its diff:
```python
import functools

import jax
import jax.numpy as jnp
from jax import lax
from jax.experimental import pallas as pl
from jax.experimental.pallas import tpu as pltpu
from jax.sharding import PartitionSpec as P

EPSILON = 1e-06
LANES = 128
GROUP = 16
LEAD = 6
TILES = 8
STEP = 4
F32 = jnp.float32
BF16 = jnp.bfloat16
MESH = pl.DeviceIdType.MESH


def iota(shape, dim):
    return lax.broadcasted_iota(jnp.int32, shape, dim)


def skewed(row):
    return pltpu.roll(jnp.broadcast_to(row, (LANES, LANES)), 0, 1, stride=1, stride_axis=0)


def tile_lanes(tile):
    return pl.ds(pl.multiple_of(tile * LANES, LANES), LANES)


def hyena_kernel(
    n_ctx, n_tp, full_width,
    order_ref, prev_ref, q_hbm, k_hbm, v_hbm, q_two_hbm, k_two_hbm, short_ref, medium_ref, long_ref, gain_ref,
    out_ref,
    q_in, k_in, v_in, q_two, k_two, taps, turned, signal, edge, q_feat, k_head, v_head, z_pad, medium_toe, long_toe, long_f32,
    send_one, recv_one, send_two, recv_two, send_u, recv_u, part, part_recv, scale, scale_recv, spread, total, in_order, send_y, recv_y,
    in_sem, one_send, one_recv, two_send, two_recv, u_send, u_recv, part_send, part_sem, scale_send, scale_sem, y_send, y_recv,
):
    rows, width = q_in.shape
    me = lax.axis_index("ctx")
    my_tp = lax.axis_index("tp")
    my_group = me // TILES

    def peer(i):
        return lax.rem(me + i, n_ctx)

    barrier = pltpu.get_barrier_semaphore()

    def greet(i, carry):
        pl.semaphore_signal(barrier, inc=1, device_id={"ctx": peer(i)}, device_id_type=MESH)
        return carry

    lax.fori_loop(1, n_ctx, greet, 0)
    for i in range(1, n_tp):
        pl.semaphore_signal(barrier, inc=1, device_id={"tp": lax.rem(my_tp + i, n_tp)}, device_id_type=MESH)

    loads = [
        pltpu.make_async_copy(src, dst, in_sem.at[i])
        for i, (src, dst) in enumerate(((q_hbm, q_in), (k_hbm, k_in), (v_hbm, v_in), (q_two_hbm, q_two), (k_two_hbm, k_two)))
    ]
    for load in loads:
        load.start()

    groups = short_ref.shape[2]
    pick = (iota((groups, width), 0) == iota((groups, width), 1) // GROUP).astype(F32)
    for which in range(3):
        taps[which, 0 : LEAD + 1, :] = jnp.dot(short_ref[which].astype(F32), pick, preferred_element_type=F32)
    flip = (iota((LANES, LANES), 0) == (LANES - iota((LANES, LANES), 1)) % LANES).astype(F32)
    turned[...] = jnp.dot(medium_ref[...].astype(F32), flip, preferred_element_type=F32)
    long_f32[...] = long_ref[...].astype(F32)
    edge[...] = jnp.zeros(edge.shape, F32)
    signal[0:8, :] = jnp.zeros((8, LANES), F32)
    spread[0 : STEP * GROUP, :] = jnp.zeros((STEP * GROUP, spread.shape[1]), BF16)
    for load in loads[:3]:
        load.wait()

    def local_step(tile, carry):
        lanes = tile_lanes(tile)
        features = []
        for which, ref in enumerate((q_in, k_in, v_in)):
            signal[8 : 8 + rows, :] = ref[:, lanes].astype(F32)
            tap = taps[which, :, lanes]
            feature = jnp.zeros((rows, LANES), F32)
            for j in range(LEAD + 1):
                feature += signal[8 - j : 8 - j + rows, :] * tap[j : j + 1]
            features.append(feature)
        q_feat[tile] = features[0]
        k_head[tile] = features[1][:GROUP]
        v_head[tile] = features[2][:GROUP]
        z_pad[tile, LANES : LANES + rows, :] = (features[1] * features[2]).astype(BF16)
        ends = [ref[rows - 8 :, lanes].astype(F32)[8 - LEAD :] for ref in (q_in, k_in, v_in)]
        ends = jnp.concatenate(ends + [jnp.zeros((6, LANES), F32)], axis=0)
        for a in range(TILES):
            send_one[a * TILES + tile, 0:16, :] = z_pad[tile, rows + 16 * a : rows + 16 * a + 16, :]
            long_row = long_f32[pl.ds(a * TILES + tile, 1), :]
            piece = [ends[3 * a : 3 * a + 3], long_row[:, :LANES], long_row[:, LANES:], jnp.zeros((3, LANES), F32)]
            send_one[a * TILES + tile, 16:24, :] = jnp.concatenate(piece, axis=0).astype(BF16)
        return carry

    lax.fori_loop(0, TILES, local_step, 0)
    pl.semaphore_wait(barrier, n_ctx - 1 + n_tp - 1)

    def send_all(source, target, send_sem, recv_sem):
        def send(i, carry):
            p = peer(i)
            pltpu.make_async_remote_copy(
                source.at[p], target.at[me], send_sem, recv_sem, device_id={"ctx": p}, device_id_type=MESH
            ).start()
            return carry

        lax.fori_loop(1, n_ctx, send, 0)

    def wait_for(ref, count, sem):
        view = ref.at[pl.ds(0, count)]
        pltpu.make_async_copy(view, view, sem).wait()

    send_all(send_one, recv_one, one_send, one_recv)
    recv_one[me] = send_one[me]

    row_at, col_at = iota((LANES, LANES), 0), iota((LANES, LANES), 1)

    def medium_step(tile, carry):
        for g in range(TILES):
            skew = skewed(turned[pl.ds(tile * TILES + g, 1), :])
            at = pl.ds(g * LANES, LANES)
            medium_toe[tile, at, 0:LANES] = jnp.where(col_at > row_at, skew, 0.0).astype(BF16)
            medium_toe[tile, at, LANES : 2 * LANES] = jnp.where(col_at <= row_at, skew, 0.0).astype(BF16)
        return carry

    lax.fori_loop(0, TILES, medium_step, 0)

    wait_for(recv_one, n_ctx - 1, one_recv)

    def route(d, carry):
        send_two[d] = recv_one[prev_ref[order_ref[d]]]
        return carry

    lax.fori_loop(0, n_ctx, route, 0)
    recv_two[me] = recv_one[prev_ref[order_ref[me]]]
    send_all(send_two, recv_two, two_send, two_recv)

    long_toe[:, 0:LANES] = jnp.zeros((LANES, LANES), BF16)

    def long_step(k, last):
        row = recv_one[k, 16:24, :].astype(F32)
        first, second = skewed(row[3:4]), skewed(row[4:5])
        at = pl.multiple_of(LANES + k * rows, LANES)
        long_toe[:, pl.ds(at, LANES)] = jnp.where(col_at >= row_at, first, last).astype(BF16)
        long_toe[:, pl.ds(at + LANES, LANES)] = jnp.where(col_at >= row_at, second, first).astype(BF16)
        return second

    lax.fori_loop(0, n_ctx, long_step, jnp.zeros((LANES, LANES), F32))
    loads[3].wait()
    loads[4].wait()
    wait_for(recv_two, n_ctx - 1, two_recv)

    before = jnp.minimum(order_ref[me], 1).astype(F32)
    owner = iota((LANES, 2 * LANES), 1) % LANES // GROUP

    def mix_step(i, energy):
        tile = lax.rem(my_group + i, TILES)
        lanes = tile_lanes(tile)
        ends = jnp.concatenate([recv_two[a * TILES + tile, 16:24, :].astype(F32)[:3] for a in range(6)], axis=0) * before
        heads = []
        for which, head in enumerate((q_feat[tile, 0:GROUP, :], k_head[tile], v_head[tile])):
            edge[0:8, :] = jnp.concatenate([jnp.zeros((8 - LEAD, LANES), F32), ends[which * LEAD : (which + 1) * LEAD]], axis=0)
            tap = taps[which, :, lanes]
            for j in range(LEAD + 1):
                head += edge[8 - j : 8 - j + GROUP, :] * tap[j : j + 1]
            heads.append(head)
        q_feat[tile, 0:GROUP, :] = heads[0]
        z_pad[tile, LANES : LANES + GROUP, :] = (heads[1] * heads[2]).astype(BF16)
        for a in range(TILES):
            z_pad[tile, 16 * a : 16 * a + 16, :] = (recv_two[a * TILES + tile, 0:16, :].astype(F32) * before).astype(BF16)
        stacked = jnp.concatenate([z_pad[tile, 0:rows, :], z_pad[tile, LANES : LANES + rows, :]], axis=1)
        product = jnp.dot(medium_toe[tile], stacked, preferred_element_type=F32)
        medium = jnp.zeros((LANES, 2 * LANES), F32)
        for g in range(TILES):
            medium = jnp.where(owner == g, product[g * LANES : (g + 1) * LANES], medium)
        medium = jnp.concatenate([medium[:, :LANES], medium[:, LANES:]], axis=0)
        mixed = q_feat[tile] * medium
        sent = jnp.transpose(mixed * k_two[:, lanes].astype(F32)).astype(BF16)
        send_u[pl.ds(tile * TILES, TILES)] = sent.reshape(TILES, GROUP, rows)
        energy = energy + mixed * mixed

        def send(j, carry):
            p = tile * TILES + lax.rem(me + j, TILES)

            @pl.when(p != me)
            def _():
                pltpu.make_async_remote_copy(
                    send_u.at[p], recv_u.at[me], u_send, u_recv, device_id={"ctx": p}, device_id_type=MESH
                ).start()

            return carry

        lax.fori_loop(0, TILES, send, 0)
        return energy

    energy = lax.fori_loop(0, width // LANES, mix_step, jnp.zeros((rows, LANES), F32))
    recv_u[me] = send_u[me]

    part[...] = jnp.sum(jnp.transpose(energy), axis=0, keepdims=True)
    for i in range(1, n_tp):
        pltpu.make_async_remote_copy(
            part, part_recv.at[i - 1], part_send, part_sem, device_id={"tp": lax.rem(my_tp + i, n_tp)}, device_id_type=MESH
        ).start()
    wait_for(part_recv, n_tp - 1, part_sem)
    whole = part[...]
    for i in range(1, n_tp):
        whole = whole + part_recv[i - 1]
    scale[...] = lax.rsqrt(whole / full_width + EPSILON)
    scale_recv[me] = scale[...]

    def send_scale(i, carry):
        p = peer(i)
        pltpu.make_async_remote_copy(
            scale, scale_recv.at[me], scale_send, scale_sem, device_id={"ctx": p}, device_id_type=MESH
        ).start()
        return carry

    lax.fori_loop(1, n_ctx, send_scale, 0)
    gain_row = jnp.broadcast_to(gain_ref[pl.ds(my_group, 1), :], (GROUP, LANES))
    gain_at = iota((GROUP, LANES), 1) == lax.rem(me, TILES) * GROUP + iota((GROUP, LANES), 0)
    gain = jnp.sum(jnp.where(gain_at, gain_row, 0.0), axis=1, keepdims=True)
    wait_for(recv_u, n_ctx - 1, u_recv)
    wait_for(scale_recv, n_ctx - 1, scale_sem)

    def place(b, carry):
        holder = prev_ref[lax.rem(b + 1, n_ctx)]
        value = (recv_u[holder].astype(F32) * scale_recv[holder]).astype(BF16)
        total[pl.ds(pl.multiple_of(b * GROUP, GROUP), GROUP), :] = value.astype(F32) * gain
        for s in range(STEP):
            spread[pl.ds(pl.multiple_of((b + s) * GROUP, GROUP), GROUP), s * rows : (s + 1) * rows] = value
        return carry

    lax.fori_loop(0, n_ctx, place, 0)
    for n in range(n_ctx // STEP):
        count = (n_ctx - n * STEP) * GROUP
        band = []
        for s in range(STEP):
            at = LANES + (n * STEP + s) * rows
            band += [long_toe[:, at : at + rows], long_toe[:, at - LANES : at - LANES + rows]]
        total[n * STEP * GROUP :, :] += jnp.dot(spread[0:count, :], jnp.concatenate(band, axis=0), preferred_element_type=F32)

    in_order[...] = total[...].astype(BF16).reshape(in_order.shape)

    def give(d, carry):
        send_y[d] = in_order[order_ref[d]]
        return carry

    lax.fori_loop(0, n_ctx, give, 0)

    def send_back(i, carry):
        p = peer(i)
        pltpu.make_async_remote_copy(
            send_y.at[p], recv_y.at[me], y_send, y_recv.at[my_group], device_id={"ctx": p}, device_id_type=MESH
        ).start()
        return carry

    lax.fori_loop(1, n_ctx, send_back, 0)
    recv_y[me] = send_y[me]

    def gate(tile):
        lanes = tile_lanes(tile)
        piece = recv_y[pl.ds(tile * TILES, TILES)].astype(F32).reshape(LANES, rows)
        out_ref[:, lanes] = (jnp.transpose(piece) * q_two[:, lanes].astype(F32)).astype(BF16)

    def gate_step(i, carry):
        tile = lax.rem(my_group + TILES - i, TILES)
        wait_for(recv_y, TILES, y_recv.at[tile])
        gate(tile)
        return carry

    lax.fori_loop(1, TILES, gate_step, 0)
    wait_for(recv_y, TILES - 1, y_recv.at[my_group])
    gate(my_group)
    wait_for(send_one, n_ctx - 1, one_send)
    wait_for(send_two, n_ctx - 1, two_send)
    wait_for(send_u, n_ctx - 1, u_send)
    wait_for(part_recv, n_tp - 1, part_send)
    wait_for(scale_recv, n_ctx - 1, scale_send)
    wait_for(send_y, n_ctx - 1, y_send)


def per_device(q_one, k_one, v_one, q_two, k_two, short_taps, medium_taps, long_taps, skip_gain, block_order, prev_owner):
    rows, width = q_one.shape
    n_ctx, n_tp = lax.axis_size("ctx"), lax.axis_size("tp")
    span = n_ctx * rows
    VM, SM, ANY = (pl.BlockSpec(memory_space=s) for s in (pltpu.VMEM, pltpu.SMEM, pl.ANY))
    vmem = pltpu.VMEM
    dma = pltpu.SemaphoreType.DMA
    return pl.pallas_call(
        functools.partial(hyena_kernel, n_ctx, n_tp, width * n_tp),
        out_shape=jax.ShapeDtypeStruct((rows, width), BF16),
        in_specs=[SM] * 2 + [ANY] * 5 + [VM] * 4,
        out_specs=VM,
        scratch_shapes=[vmem((rows, width), BF16)] * 5
        + [
            vmem((3, 8, width), F32),
            vmem((width // GROUP, LANES), F32),
            vmem((8 + rows, LANES), F32),
            vmem((8 + GROUP, LANES), F32),
            vmem((TILES, rows, LANES), F32),
            vmem((TILES, GROUP, LANES), F32),
            vmem((TILES, GROUP, LANES), F32),
            vmem((TILES, LANES + rows, LANES), BF16),
            vmem((TILES, TILES * LANES, 2 * LANES), BF16),
            vmem((LANES, LANES + span), BF16),
            vmem((n_ctx, rows), F32),
        ]
        + [vmem((n_ctx, 24, LANES), BF16)] * 4
        + [vmem((n_ctx, GROUP, rows), BF16)] * 2
        + [
            vmem((1, rows), F32),
            vmem((n_tp - 1, 1, rows), F32),
            vmem((1, rows), F32),
            vmem((n_ctx, 1, rows), F32),
            vmem(((n_ctx + STEP) * GROUP, STEP * rows), BF16),
            vmem((n_ctx * GROUP, rows), F32),
        ]
        + [vmem((n_ctx, GROUP, rows), BF16)] * 3
        + [dma((5,))]
        + [dma] * 11
        + [dma((TILES,))],
        compiler_params=pltpu.CompilerParams(collective_id=0, has_side_effects=True, vmem_limit_bytes=60 * 1024 * 1024),
        name="hyena",
    )(
        block_order, prev_owner, q_one, k_one, v_one, q_two, k_two,
        short_taps, jnp.transpose(medium_taps), long_taps, skip_gain.reshape(width // LANES, LANES),
    )


def solution(mesh):
    in_specs = (
        P("ctx", "tp"),
        P("ctx", "tp"),
        P("ctx", "tp"),
        P("ctx", "tp"),
        P("ctx", "tp"),
        P(None, None, "tp"),
        P(None, "tp"),
        P("tp", "ctx"),
        P("tp"),
        P(),
        P(),
    )
    return jax.shard_map(per_device, mesh=mesh, in_specs=in_specs, out_specs=P("ctx", "tp"), check_vma=False)
```

time: 166 us -> 79 us (0.48)
  waiting for transfers between devices: 42.9 us -> 0 us
  starting transfers between devices: 41.1 us -> 0 us
  Pallas kernels: 37.9 us -> 76.9 us
  blocking collectives: 30.3 us -> 0 us
  local copies, waits for them, and re-layouts: 8.39 us -> 1.87 us
  other arithmetic: 4.5 us -> 0 us
    all_to_all x4 -> x0, waiting for transfers between devices: 42.9 us -> none  [the longest x1 16.1 us: per_device(): lax.all_to_all(v_two.reshape(ctx_count, lane_width, rows), 'ctx', split_a...]
    all_to_all x4 -> x0, starting transfers between devices: 41.1 us -> none  [the longest x1 14.8 us: per_device(): lax.all_to_all(tails, 'ctx', split_axis=0, concat_axis=0, tiled=True)]
    pallas_call x4 -> x1, Pallas kernels: 37.9 us -> 76.9 us  [per_device(): pl.pallas_call(functools.partial(hyena_kernel, n_ctx, n_tp, width * n_tp)...]
    all_to_all x1 -> x0, blocking collectives: 24.7 us -> none  [per_device(): lax.all_to_all(jnp.take(mixed_seq, block_order, axis=0), 'ctx', split_axi...]
    psum x1 -> x0, blocking collectives: 5.63 us -> none  [per_device(): energy = lax.psum(energy, 'tp')]
    gather x3 -> x0, local copies, waits for them, and re-layouts: 3.06 us -> none  [the longest x1 1.63 us: per_device(): jnp.take(mixed_seq, block_order, axis=0)]
    convert_element_type x1 -> x0, other arithmetic: 2.1 us -> none  [per_device(): v_two = (mixed * lax.rsqrt(energy / full_width + EPSILON)).astype(BF16)]
    unnamed x19 -> x1, local copies, waits for them, and re-layouts: 3.46 us -> 1.87 us
  transfers between devices with their start and end apart: 4 -> 0, of which waited for: 3 -> 0; matrix products, arithmetic and copies ran while one was open for 5% -> 0% of each run, Pallas kernels for 6% -> 0%
where the time goes in v2:
time: 79 us; the launch traced here: 78.8 us
  Pallas kernels  76.9 us (97%)
  local copies, waits for them, and re-layouts  1.87 us (2%)
    pallas_call x1, Pallas kernels, per_device(): pl.pallas_call(functools.partial(hyena_kernel, n_ctx, n_tp, width * n_tp)...  76.9 us
    unnamed x1, local copies, waits for them, and re-layouts  1.87 us

profile of v2, /device:TPU:2, one launch (start us, length us, event | category | flops | bytes accessed | tf_op | source)
XLA Modules:
  0.0 78.8 jit_solution(9217463644142615808)
XLA Ops:
  0.0 76.9 %hyena.1 = bf16[256,1024]{1,0:T(8,128)(2,1)} custom-call(s32[64]{0:T(128)} %order_ref.1, s32[64]{0:T(128)} %prev_ref.1, bf16[256,1024]{1,0:T(8,128)(2,1)} %q_hbm.1, bf16[256,1024]{1,0:T(8,128)(2,1)} %k_hbm.1, bf16[256,1024]{1,0:T(8,128)(2,1)} %v_hbm.1, bf16[256,1024]{1,0:T(8,128)(2,1)} %q_two_hbm.1, bf16[256,1024]{1,0:T(8,128)(2,1)} %k_two_hbm.1, ...), custom_call_target="tpu_custom_call" | custom-call | tf_op jit(solution)/shard_map/hyena/pallas_call | solution.py:295
  76.9 1.9 %copy.13 = bf16[256,1024]{1,0:T(8,128)(2,1)} copy(bf16[256,1024]{1,0:T(8,128)(2,1)} %hyena.1) | data formatting | bytes 1048576
